TPU v7x, 32 devices: a whole 2x2x4 slice. The times are simulated.
32 devices in a mesh: groups: 2 (over y), ctx: 4 (over x, core), mp: 4 (over z).
Axes of the slice: x: 2, y: 2, z: 4, core: 2. Of those that a mesh axis runs over, the one named last changes fastest.
Arguments:
- tokens: bfloat16 [3072, 8192], P(('groups', 'ctx')), parts along dimension 0, may hold values from -6 to 6
- norm_gain: bfloat16 [8192], replicated, may hold values from 0.099609375 to 1.8984375
- w_query: bfloat16 [8192, 4096], P('ctx', 'mp'), may hold values from -0.44194174 to 0.44194174
- w_key: bfloat16 [8192, 1024], P('ctx', 'mp'), may hold values from -0.044194174 to 0.044194174
- value_weight: bfloat16 [8192, 1024], P('ctx', 'mp'), may hold values from -0.0625 to 0.0625
- slab_order: int32 [8], P('groups'), parts along dimension 0, may hold values from 0 to 3, each once
- segment_ids: int32 [3072], P('groups'), parts along dimension 0, may hold values from 0 to 3, as said below
Outputs:
- attended: bfloat16 [3072, 4096], P(('groups', 'ctx'), 'mp'), parts along dimension 0
There are 2 independent parts, one for each index of `groups`. A program takes and returns all parts, laid end to end along the dimension named above; an argument that names none is the same for every part. Nothing has to cross between parts.
Inputs may be any that keep to these rules, and one draw needn't show every extreme that they name: `segment_ids`: never falling along positions; each of the 4 segments holds at least one position.
All inputs are finite; a program needn't handle non-finite values.
Results may differ from a plain program's by a relative error of at most 0.012.
Values may be sent and summed in bfloat16 or wider, within the bound.
A program may use at most 128 MiB of HBM per device.

v0:
```python
import math

import jax
import jax.numpy as jnp
from jax import lax
from jax.sharding import PartitionSpec as P

HEAD_SIZE = 128


def apply_rotary(values, positions, heads):
    width = values.shape[1] // heads
    half = width // 2
    freqs = jnp.exp(jnp.arange(half, dtype=jnp.float32) * (-2.0 * math.log(500000.0) / width))
    angles = positions.astype(jnp.float32)[:, None] * freqs[None, :]
    cosine = jnp.cos(angles)[:, None, :]
    sine = jnp.sin(angles)[:, None, :]
    shaped = values.reshape(values.shape[0], heads, width)
    first = shaped[..., :half]
    second = shaped[..., half:]
    turned = jnp.concatenate(
        [first * cosine - second * sine, second * cosine + first * sine], axis=-1
    )
    return turned.reshape(values.shape)


def local(tokens, norm_gain, w_query, w_key, value_weight, slab_order, segment_ids):
    tok_rows = tokens.shape[0]
    device_slab = lax.axis_index("ctx")
    position_all = (
        slab_order[:, None] * tok_rows + jnp.arange(tok_rows, dtype=jnp.int32)[None, :]
    ).reshape(-1)
    segment_all = jnp.take(segment_ids, position_all)
    my_position = lax.dynamic_slice_in_dim(position_all, device_slab * tok_rows, tok_rows)
    my_segment = lax.dynamic_slice_in_dim(segment_all, device_slab * tok_rows, tok_rows)
    floats = tokens.astype(jnp.float32)
    inverse = lax.rsqrt(jnp.mean(floats * floats, axis=-1, keepdims=True) + 1e-05)
    normed = (floats * inverse * norm_gain.astype(jnp.float32)[None, :]).astype(jnp.bfloat16)
    query_cols = w_query.shape[1]
    key_cols = w_key.shape[1]
    query = jnp.dot(
        normed,
        lax.all_gather(w_query, "ctx", axis=0, tiled=True),
        preferred_element_type=jnp.float32,
    )
    key_projected = jnp.dot(
        normed, lax.all_gather(w_key, "ctx", axis=0, tiled=True), preferred_element_type=jnp.float32
    )
    value_proj = jnp.dot(
        normed,
        lax.all_gather(value_weight, "ctx", axis=0, tiled=True),
        preferred_element_type=jnp.float32,
    )
    head_size = HEAD_SIZE
    heads_here = query_cols // head_size
    kv_here = key_cols // head_size
    group_width = heads_here // kv_here
    query_rot = (
        apply_rotary(query, my_position, heads_here)
        .astype(jnp.bfloat16)
        .reshape(tok_rows, kv_here, group_width, head_size)
    )
    key_rotary = apply_rotary(key_projected, my_position, kv_here).astype(jnp.bfloat16)
    value_b = value_proj.astype(jnp.bfloat16)
    scale = head_size ** (-0.5)
    start_state = (
        jnp.full((kv_here, group_width, tok_rows), -1e30, jnp.float32),
        jnp.zeros((kv_here, group_width, tok_rows), jnp.float32),
        jnp.zeros((kv_here, group_width, tok_rows, head_size), jnp.float32),
    )
    state = start_state
    key_piece = lax.all_gather(key_rotary, "ctx", axis=0, tiled=True)
    value_piece = lax.all_gather(value_b, "ctx", axis=0, tiled=True)
    piece_rows = key_piece.shape[0]
    block_rows = math.gcd(piece_rows, 1024)
    block_count = piece_rows // block_rows
    key_blocks = key_piece.reshape(block_count, block_rows, kv_here, head_size)
    value_blocks = value_piece.reshape(block_count, block_rows, kv_here, head_size)
    key_positions = position_all.reshape(block_count, block_rows)
    key_segments = segment_all.reshape(block_count, block_rows)

    def advance(inner, item):
        key_block, value_block, block_positions, block_segments = item
        allowed = (block_positions[None, :] <= my_position[:, None]) & (
            block_segments[None, :] == my_segment[:, None]
        )
        running_max, running_sum, running_acc = inner
        scores = (
            jnp.einsum("tkgd,nkd->kgtn", query_rot, key_block, preferred_element_type=jnp.float32)
            * scale
        )
        scores = jnp.where(allowed[None, None], scores, -1e30)
        new_max = jnp.maximum(running_max, jnp.max(scores, axis=-1))
        exps = jnp.where(allowed[None, None], jnp.exp(scores - new_max[..., None]), 0.0)
        factor = jnp.exp(running_max - new_max)
        new_sum = running_sum * factor + jnp.sum(exps, axis=-1)
        new_acc = running_acc * factor[..., None] + jnp.einsum(
            "kgtn,nkd->kgtd",
            exps.astype(jnp.bfloat16),
            value_block,
            preferred_element_type=jnp.float32,
        )
        inner = (new_max, new_sum, new_acc)
        return (inner, None)

    state, _ = lax.scan(advance, state, (key_blocks, value_blocks, key_positions, key_segments))
    final_max, final_sum, final_acc = state
    mixed = final_acc / final_sum[..., None]
    return (
        jnp.transpose(mixed, (2, 0, 1, 3))
        .reshape(tok_rows, heads_here * head_size)
        .astype(jnp.bfloat16)
    )


def solution(mesh):
    return jax.shard_map(
        local,
        mesh=mesh,
        in_specs=(
            P(("groups", "ctx"), None),
            P(),
            P("ctx", "mp"),
            P("ctx", "mp"),
            P("ctx", "mp"),
            P("groups"),
            P("groups"),
        ),
        out_specs=P(("groups", "ctx"), "mp"),
        check_vma=False,
    )
```

profile of v0, /device:TPU:0, one launch (start us, length us, event | category | flops | bytes accessed | tf_op | source)
XLA Modules:
  0.0 256.6 jit_solution(9475699111471552098)
XLA Ops:
  6.5 0.7 all-gather.4.cloned.1.call-update
  7.3 0.7 all-gather.8.cloned.1.call-update
  8.1 0.7 all-gather.6.cloned.1.call-update
  8.8 0.1 fusion.19
  8.9 0.1 fusion.24
  9.0 0.4 multiply_cosine_fusion
  9.4 0.1 copy.16
  9.6 0.1 copy.17
  9.8 8.4 %gather_fusion = s32[1536]{0:T(1024)S(1)} fusion(s32[1536]{0:T(1024)S(1)} %copy-done, s32[2048]{0:T(1024)S(1)} %pad_clamp_fusion), kind=kCustom, calls=%fused_computation | custom fusion | bytes 18432 | tf_op jit(solution)/shard_map/jit(_take)/gather | solution.py:33
  18.2 5.0 %fusion.14 = f32[384]{0:T(512)S(1)} fusion(bf16[384,8192]{1,0:T(8,128)(2,1)} %param.9), kind=kLoop, calls=%fused_computation.27 | loop fusion | flops 9436800 | bytes 6292992 | tf_op jit(solution)/shard_map/reduce_sum | solution.py:37
  23.2 0.1 dynamic-slice_select_fusion
  23.3 22.8 %all-gather.4.cloned.1.call-done = bf16[8192,256]{1,0:T(8,128)(2,1)} async-done(((bf16[2048,256]{1,0:T(8,128)(2,1)}), bf16[8192,256]{1,0:T(8,128)(2,1)}) %all-gather.4.cloned.1.call-update) | async-done | bytes 4194320 | tf_op jit(solution)/shard_map/all_gather | solution.py:47
  46.1 6.6 %fusion.22 = f32[384,256]{0,1:T(8,128)S(1)} fusion(bf16[8192,256]{1,0:T(8,128)(2,1)} %all-gather.4.cloned.1.call-done, bf16[384,8192]{1,0:T(8,128)(2,1)} %param.9, f32[8192]{0:T(1024)S(1)} %convert_element_type.38, f32[384]{0:T(512)S(1)} %add_rsqrt_fusion), kind=kOutput, calls=%fused_computation.54 | convolution fusion | flops 1623195648 | bytes 10913280 | tf_op jit(solution)/shard_map/dot_general | solution.py:46
  52.8 0.1 copy.25
  53.0 11.9 %all_gather.16 = bf16[1536,256]{1,0:T(8,128)(2,1)S(1)} all-gather(bf16[384,256]{1,0:T(8,128)(2,1)S(1)} %copy.25), channel_id=1, replica_groups=mesh['groups'=2,'ctx'=4,'mp'=4] {'ctx'}, dimensions={0}, use_global_device_ids=true | all-gather | bytes 983040 | tf_op jit(solution)/shard_map/all_gather | solution.py:72
  64.9 0.2 reshape.188
  65.1 19.7 %all-gather.8.cloned.1.call-done = bf16[8192,256]{1,0:T(8,128)(2,1)} async-done(((bf16[2048,256]{1,0:T(8,128)(2,1)}), bf16[8192,256]{1,0:T(8,128)(2,1)}) %all-gather.8.cloned.1.call-update) | async-done | bytes 4194320 | tf_op jit(solution)/shard_map/all_gather | solution.py:51
  84.8 5.9 %convolution_convert_fusion = bf16[384,256]{1,0:T(8,128)(2,1)S(1)} fusion(bf16[8192,256]{1,0:T(8,128)(2,1)} %all-gather.8.cloned.1.call-done, bf16[384,8192]{1,0:T(8,128)(2,1)} %param.9, f32[8192]{0:T(1024)S(1)} %convert_element_type.38, f32[384]{0:T(512)S(1)} %add_rsqrt_fusion), kind=kOutput, calls=%fused_computation.34 | convolution fusion | flops 1623293952 | bytes 10716672 | tf_op jit(solution)/shard_map/dot_general | solution.py:49
  90.7 8.8 %all_gather.19 = bf16[1536,256]{1,0:T(8,128)(2,1)S(1)} all-gather(bf16[384,256]{1,0:T(8,128)(2,1)S(1)} %convolution_convert_fusion), channel_id=1, replica_groups=mesh['groups'=2,'ctx'=4,'mp'=4] {'ctx'}, dimensions={0}, use_global_device_ids=true | all-gather | bytes 983040 | tf_op jit(solution)/shard_map/all_gather | solution.py:73
  99.5 0.2 reshape.190
  99.7 92.7 %all-gather.6.cloned.1.call-done = bf16[8192,1024]{1,0:T(8,128)(2,1)} async-done(((bf16[2048,1024]{1,0:T(8,128)(2,1)}), bf16[8192,1024]{1,0:T(8,128)(2,1)}) %all-gather.6.cloned.1.call-update) | async-done | bytes 16777232 | tf_op jit(solution)/shard_map/all_gather | solution.py:43
  192.3 12.4 %convolution_bitcast_fusion = f32[48,8,8,128]{3,1,2,0:T(8,128)S(1)} fusion(bf16[8192,1024]{1,0:T(8,128)(2,1)} %all-gather.6.cloned.1.call-done, bf16[384,8192]{1,0:T(8,128)(2,1)} %param.9, f32[8192]{0:T(1024)S(1)} %convert_element_type.38, f32[384]{0:T(512)S(1)} %add_rsqrt_fusion), kind=kOutput, calls=%fused_computation.33 | convolution fusion | flops 6455033856 | bytes 24675840 | tf_op jit(solution)/shard_map/dot_general | solution.py:41
  204.7 0.3 copy.29
  205.1 0.7 subtract_convert_fusion
  205.7 0.4 pad_maximum_fusion
  206.2 0.1 copy.18
  206.3 39.8 %while.15 = (s32[]{:T(128)}, f32[2,4,384]{2,1,0:T(4,128)S(1)}, f32[2,4,384]{2,1,0:T(4,128)S(1)}, f32[2,4,384,128]{3,2,1,0:T(8,128)}, s32[3,512]{1,0:T(4,128)S(1)...) while((s32[]{:T(128)}, f32[2,4,384]{2,1,0:T(4,128)S(1)}, ...), condition=%wide.region_4.5_spmd.clone, body=%wide.region_1.0_spmd.clone.sunk | while | flops 827538432 | bytes 50543788 | solution.py:106
  206.3 0.2 compare_and_fusion.2
  206.6 0.4 constant_dynamic-slice_fusion.7
  206.9 3.8 %fusion.37 = (f32[2,4,384]{2,1,0:T(4,128)S(1)}, f32[2,512,384,4]{2,1,3,0:T(8,128)}) fusion(pred[384,512]{0,1:T(8,128)(4,1)S(1)} %compare_and_fusion.2, bf16[384,2,4,128]{3,0,2,1:T(8,128)(2,1)S(1)} %get-tuple-element.281, bf16[1,512,2,128]{3,2,1,0:T(2,128)(2,1)S(1)} %get-tuple-element.240), kind=kOutput, calls=%fused_computation.3.clone.1 | convolution fusion | flops 407368704 | bytes 7548928 | tf_op jit(solution)/shard_map/while/body/eval_jaxpr/tkgd,nkd->kgtn/dot_general | solution.py:89
  210.8 4.4 %fusion.38 = f32[2,4,384]{2,1,0:T(4,128)S(1)} fusion(f32[2,512,384,4]{2,1,3,0:T(8,128)} %get-tuple-element.242, f32[2,4,384]{2,1,0:T(4,128)S(1)} %select_maximum_fusion.2, pred[384,512]{0,1:T(8,128)(4,1)S(1)} %compare_and_fusion.2), kind=kLoop, calls=%fused_computation.5.clone.1 | loop fusion | flops 7861248 | bytes 6512640 | tf_op jit(solution)/shard_map/while/body/eval_jaxpr/reduce_sum | solution.py:96
  215.3 0.1 copy-done.1
  215.4 3.4 %fusion.40 = f32[2,4,384,128]{3,2,1,0:T(8,128)} fusion(f32[2,4,384,128]{3,2,1,0:T(8,128)} %get-tuple-element.262, f32[2,512,384,4]{2,1,3,0:T(8,128)S(1)} %copy-done.1, f32[2,4,384]{2,1,0:T(4,128)S(1)} %select_maximum_fusion.2, pred[384,512]{0,1:T(8,128)(4,1)S(1)} %compare_and_fusion.2, f32[2,4,384]{2,1,0:T(4,128)S(1)} %get-tuple-element.244, ...), kind=kOutput, calls=%fused_computation.9.clone.1 | convolution fusion | flops 411697152 | bytes 9920513 | tf_op jit(solution)/shard_map/while/body/eval_jaxpr/kgtn,nkd->kgtd/dot_general | solution.py:97
  218.8 0.2 compare_and_fusion.2
  219.1 0.4 constant_dynamic-slice_fusion.7
  219.4 3.9 %fusion.37 = (f32[2,4,384]{2,1,0:T(4,128)S(1)}, f32[2,512,384,4]{2,1,3,0:T(8,128)}) fusion(pred[384,512]{0,1:T(8,128)(4,1)S(1)} %compare_and_fusion.2, bf16[384,2,4,128]{3,0,2,1:T(8,128)(2,1)S(1)} %get-tuple-element.281, bf16[1,512,2,128]{3,2,1,0:T(2,128)(2,1)S(1)} %get-tuple-element.240), kind=kOutput, calls=%fused_computation.3.clone.1 | convolution fusion | flops 407368704 | bytes 7548928 | tf_op jit(solution)/shard_map/while/body/eval_jaxpr/tkgd,nkd->kgtn/dot_general | solution.py:89
  223.3 4.4 %fusion.38 = f32[2,4,384]{2,1,0:T(4,128)S(1)} fusion(f32[2,512,384,4]{2,1,3,0:T(8,128)} %get-tuple-element.242, f32[2,4,384]{2,1,0:T(4,128)S(1)} %select_maximum_fusion.2, pred[384,512]{0,1:T(8,128)(4,1)S(1)} %compare_and_fusion.2), kind=kLoop, calls=%fused_computation.5.clone.1 | loop fusion | flops 7861248 | bytes 6512640 | tf_op jit(solution)/shard_map/while/body/eval_jaxpr/reduce_sum | solution.py:96
  227.8 0.1 copy-done.1
  227.9 4.6 %fusion.40 = f32[2,4,384,128]{3,2,1,0:T(8,128)} fusion(f32[2,4,384,128]{3,2,1,0:T(8,128)} %get-tuple-element.262, f32[2,512,384,4]{2,1,3,0:T(8,128)S(1)} %copy-done.1, f32[2,4,384]{2,1,0:T(4,128)S(1)} %select_maximum_fusion.2, pred[384,512]{0,1:T(8,128)(4,1)S(1)} %compare_and_fusion.2, f32[2,4,384]{2,1,0:T(4,128)S(1)} %get-tuple-element.244, ...), kind=kOutput, calls=%fused_computation.9.clone.1 | convolution fusion | flops 411697152 | bytes 9920513 | tf_op jit(solution)/shard_map/while/body/eval_jaxpr/kgtn,nkd->kgtd/dot_general | solution.py:97
  232.5 0.2 compare_and_fusion.2
  232.7 0.4 constant_dynamic-slice_fusion.7
  233.1 3.8 %fusion.37 = (f32[2,4,384]{2,1,0:T(4,128)S(1)}, f32[2,512,384,4]{2,1,3,0:T(8,128)}) fusion(pred[384,512]{0,1:T(8,128)(4,1)S(1)} %compare_and_fusion.2, bf16[384,2,4,128]{3,0,2,1:T(8,128)(2,1)S(1)} %get-tuple-element.281, bf16[1,512,2,128]{3,2,1,0:T(2,128)(2,1)S(1)} %get-tuple-element.240), kind=kOutput, calls=%fused_computation.3.clone.1 | convolution fusion | flops 407368704 | bytes 7548928 | tf_op jit(solution)/shard_map/while/body/eval_jaxpr/tkgd,nkd->kgtn/dot_general | solution.py:89
  236.9 4.4 %fusion.38 = f32[2,4,384]{2,1,0:T(4,128)S(1)} fusion(f32[2,512,384,4]{2,1,3,0:T(8,128)} %get-tuple-element.242, f32[2,4,384]{2,1,0:T(4,128)S(1)} %select_maximum_fusion.2, pred[384,512]{0,1:T(8,128)(4,1)S(1)} %compare_and_fusion.2), kind=kLoop, calls=%fused_computation.5.clone.1 | loop fusion | flops 7861248 | bytes 6512640 | tf_op jit(solution)/shard_map/while/body/eval_jaxpr/reduce_sum | solution.py:96
  241.4 0.1 copy-done.1
  241.5 4.6 %fusion.40 = f32[2,4,384,128]{3,2,1,0:T(8,128)} fusion(f32[2,4,384,128]{3,2,1,0:T(8,128)} %get-tuple-element.262, f32[2,512,384,4]{2,1,3,0:T(8,128)S(1)} %copy-done.1, f32[2,4,384]{2,1,0:T(4,128)S(1)} %select_maximum_fusion.2, pred[384,512]{0,1:T(8,128)(4,1)S(1)} %compare_and_fusion.2, f32[2,4,384]{2,1,0:T(4,128)S(1)} %get-tuple-element.244, ...), kind=kOutput, calls=%fused_computation.9.clone.1 | convolution fusion | flops 411697152 | bytes 9920513 | tf_op jit(solution)/shard_map/while/body/eval_jaxpr/kgtn,nkd->kgtd/dot_general | solution.py:97
  246.1 1.9 fusion.17
  248.0 0.6 copy.21
  248.6 1.4 convert_element_type.46
  (40 shorter events, 0.4 us)
Async XLA Ops:
  6.5 3.2 %copy-start = (s32[1536]{0:T(1024)S(1)}, s32[1536]{0:T(1024)}, u32[]{:S(2)}) copy-start(s32[1536]{0:T(1024)} %param.15) | copy-start | bytes 18436
  6.5 2.2 copy-start.3
  6.5 3.1 %copy-start.2 = (bf16[8192]{0:T(1024)(128)(2,1)S(1)}, bf16[8192]{0:T(1024)(128)(2,1)}, u32[]{:S(2)}) copy-start(bf16[8192]{0:T(1024)(128)(2,1)} %param.10) | copy-start | bytes 49156
  6.5 39.6 %all-gather.4.cloned.1.call-start = ((), (), s32[]{:S(2)}) async-start(), calls=%async_computation | async-start | bytes 5242880 | tf_op jit(solution)/shard_map/all_gather | solution.py:47
  7.3 77.5 %all-gather.8.cloned.1.call-start = ((), (), s32[]{:S(2)}) async-start(), calls=%async_computation.2 | async-start | bytes 5242880 | tf_op jit(solution)/shard_map/all_gather | solution.py:51
  8.0 184.3 %all-gather.6.cloned.1.call-start = ((), (), s32[]{:S(2)}) async-start(), calls=%async_computation.1 | async-start | bytes 20971520 | tf_op jit(solution)/shard_map/all_gather | solution.py:43
  210.8 4.6 %copy-start.1 = (f32[2,512,384,4]{2,1,3,0:T(8,128)S(1)}, f32[2,512,384,4]{2,1,3,0:T(8,128)}, u32[]{:S(2)}) copy-start(f32[2,512,384,4]{2,1,3,0:T(8,128)} %get-tuple-element.242) | copy-start | bytes 18874372 | tf_op jit(solution)/shard_map/while
  223.3 4.6 %copy-start.1 = (f32[2,512,384,4]{2,1,3,0:T(8,128)S(1)}, f32[2,512,384,4]{2,1,3,0:T(8,128)}, u32[]{:S(2)}) copy-start(f32[2,512,384,4]{2,1,3,0:T(8,128)} %get-tuple-element.242) | copy-start | bytes 18874372 | tf_op jit(solution)/shard_map/while
  236.9 4.6 %copy-start.1 = (f32[2,512,384,4]{2,1,3,0:T(8,128)S(1)}, f32[2,512,384,4]{2,1,3,0:T(8,128)}, u32[]{:S(2)}) copy-start(f32[2,512,384,4]{2,1,3,0:T(8,128)} %get-tuple-element.242) | copy-start | bytes 18874372 | tf_op jit(solution)/shard_map/while
Sparse Core Ops, SparseCore 0:
  8.9 37.1 all-gather.3
  47.7 37.0 all-gather.7
  86.4 105.9 all-gather.5
where the time goes:
time: 257 us
  waiting for transfers between devices  137 us (53%)
  matrix products  48.9 us (19%)
  other arithmetic  22.9 us (9%)
  blocking collectives  20.7 us (8%)
  between operations  13.3 us (5%)
  local copies, waits for them, and re-layouts  13.2 us (5%)
    all_gather x1, waiting for transfers between devices, local(): lax.all_gather(w_query, 'ctx', axis=0, tiled=True)  92.7 us
    all_gather x1, waiting for transfers between devices, local(): lax.all_gather(w_key, 'ctx', axis=0, tiled=True)  22.8 us
    all_gather x1, waiting for transfers between devices, local(): lax.all_gather(value_weight, 'ctx', axis=0, tiled=True)  19.7 us
    reduce_sum x3, other arithmetic, advance(): new_sum = running_sum * factor + jnp.sum(exps, axis=-1)  13.3 us
    dot_general x3, matrix products, advance(): jnp.einsum('kgtn,nkd->kgtd', exps.astype(jnp.bfloat16), value_block, pref...  12.5 us
    dot_general x1, matrix products, local(): jnp.dot(normed, lax.all_gather(w_query, 'ctx', axis=0, tiled=True), prefe...  12.4 us
    all_gather x1, blocking collectives, local(): key_piece = lax.all_gather(key_rotary, 'ctx', axis=0, tiled=True)  11.9 us
    dot_general x3, matrix products, advance(): jnp.einsum('tkgd,nkd->kgtn', query_rot, key_block, preferred_element_type...  11.5 us
  transfers between devices with their start and end apart: 3, of which 3 were waited for; matrix products, arithmetic and copies ran while one was open for 11% of the time, Pallas kernels for 0%

commit v1 on v0

--- a/solution.py
+++ b/solution.py
@@ -3,6 +3,8 @@
 import jax
 import jax.numpy as jnp
 from jax import lax
+from jax.experimental import pallas as pl
+from jax.experimental.pallas import tpu as pltpu
 from jax.sharding import PartitionSpec as P
 
 HEAD_SIZE = 128
@@ -24,7 +26,7 @@
     return turned.reshape(values.shape)
 
 
-def local(tokens, norm_gain, w_query, w_key, value_weight, slab_order, segment_ids):
+def local_plain(tokens, norm_gain, w_query, w_key, value_weight, slab_order, segment_ids):
     tok_rows = tokens.shape[0]
     device_slab = lax.axis_index("ctx")
     position_all = (
@@ -113,7 +115,293 @@
     )
 
 
+BLOCK = 256
+NEG = -1e30
+
+
+def fused_kernel(
+    tokens, gain, w_query, w_key, w_value, table, bounds, kpos, out,
+    wall, normed, acc, qrot, kv, lsem, cs, cr, xs, xr, ys, yr, fs, fr, hs, hr, kvs, kvr,
+):
+    g = lax.axis_index("groups")
+    t = lax.axis_index("ctx")
+    m = lax.axis_index("mp")
+    x_index = t // 2
+    core = t % 2
+    t_core = x_index * 2 + (1 - core)
+    t_x = (1 - x_index) * 2 + core
+    t_diag = (1 - x_index) * 2 + (1 - core)
+    shard_rows = w_query.shape[0]
+    half = shard_rows // 2
+    rows = tokens.shape[0]
+    kv_cols = w_key.shape[1]
+    blocks = wall.shape[0]
+    kv_heads = kv_cols // HEAD_SIZE
+    group_width = w_query.shape[1] // kv_cols
+    kv_blocks = 2 * kv_cols // BLOCK
+    core_dev = (g, t_core, m)
+    x_dev = (g, t_x, m)
+    y_dev = (1 - g, t, m)
+
+    def remote(src, dst, send, recv, dev):
+        return pltpu.make_async_remote_copy(
+            src_ref=src, dst_ref=dst, send_sem=send, recv_sem=recv,
+            device_id=dev, device_id_type=pl.DeviceIdType.MESH,
+        )
+
+    def piece(b, shard, h):
+        return wall.at[b, shard, pl.ds(pl.multiple_of(h * half, half), half), :]
+
+    def core_send(b):
+        return remote(wall.at[b, t], wall.at[b, t], cs.at[b], cr.at[b], core_dev)
+
+    def x_send(b):
+        return remote(piece(b, t, g), piece(b, t, g), xs.at[b], xr.at[b], x_dev)
+
+    def y_send(b):
+        return remote(piece(b, t_x, g), piece(b, t_x, g), ys.at[b], yr.at[b], y_dev)
+
+    def core_x(b):
+        return remote(piece(b, t_x, g), piece(b, t_x, g), fs.at[b], fr.at[b], core_dev)
+
+    def core_y(b):
+        return remote(piece(b, t_x, 1 - g), piece(b, t_x, 1 - g), hs.at[b], hr.at[b], core_dev)
+
+    def kv_copy(index, shard, dev):
+        view = kv.at[pl.ds(pl.multiple_of(shard * rows, rows), rows), :]
+        return remote(view, view, kvs.at[index], kvr.at[index], dev)
+
+    token_copy = pltpu.make_async_copy(tokens, normed, lsem.at[blocks])
+    local_copies = []
+    for b in range(blocks):
+        if b < kv_blocks // 2:
+            source = w_key.at[:, pl.ds(b * BLOCK, BLOCK)]
+        elif b < kv_blocks:
+            source = w_value.at[:, pl.ds((b - kv_blocks // 2) * BLOCK, BLOCK)]
+        else:
+            source = w_query.at[:, pl.ds((b - kv_blocks) * BLOCK, BLOCK)]
+        local_copies.append(pltpu.make_async_copy(source, wall.at[b, t], lsem.at[b]))
+    local_copies[0].start()
+    token_copy.start()
+    for copy in local_copies[1:]:
+        copy.start()
+
+    barrier = pltpu.get_barrier_semaphore()
+    for dev in (core_dev, x_dev, y_dev):
+        pl.semaphore_signal(barrier, inc=1, device_id=dev, device_id_type=pl.DeviceIdType.MESH)
+    pl.semaphore_wait(barrier, 3)
+
+    for b in range(blocks):
+        local_copies[b].wait()
+        if b < AHEAD:
+            x_send(b).start()
+            core_send(b).start()
+    token_copy.wait()
+
+    gain_row = gain[...].astype(jnp.float32)
+
+    def norm_rows(i, carry):
+        at = pl.ds(pl.multiple_of(i * 16, 16), 16)
+        floats = normed[at, :].astype(jnp.float32)
+        inverse = lax.rsqrt(jnp.mean(floats * floats, axis=-1, keepdims=True) + 1e-05)
+        normed[at, :] = (floats * inverse * gain_row).astype(jnp.bfloat16)
+        return carry
+
+    lax.fori_loop(0, rows // 16, norm_rows, 0)
+
+    def product(b, shard, h):
+        columns = pl.ds(pl.multiple_of(shard * shard_rows + h * half, half), half)
+        return jnp.dot(
+            normed[:, columns],
+            wall[b, shard, pl.ds(pl.multiple_of(h * half, half), half), :],
+            preferred_element_type=jnp.float32,
+        )
+
+    def turned(head):
+        first = acc[:, head * HEAD_SIZE : (head + 1) * HEAD_SIZE]
+        swapped = pltpu.roll(first, HEAD_SIZE // 2, 1)
+        return (first * table[0] + swapped * table[1]).astype(jnp.bfloat16)
+
+    factor = (HEAD_SIZE ** (-0.5)) * math.log2(math.e)
+    tile = 128
+
+    def attend(b):
+        heads = BLOCK // HEAD_SIZE
+        first_head = (b - kv_blocks) * heads
+
+        def one(step, carry):
+            h = step % heads
+            r = step // heads
+            at = pl.ds(pl.multiple_of(r * tile, tile), tile)
+            kv_head = (first_head + h) // group_width
+            kcol = pl.ds(pl.multiple_of(kv_head * HEAD_SIZE, HEAD_SIZE), HEAD_SIZE)
+            vcol = pl.ds(pl.multiple_of(kv_cols + kv_head * HEAD_SIZE, HEAD_SIZE), HEAD_SIZE)
+            scores = lax.dot_general(
+                qrot[at, pl.ds(pl.multiple_of(h * HEAD_SIZE, HEAD_SIZE), HEAD_SIZE)],
+                kv[:, kcol],
+                (((1,), (1,)), ((), ())),
+                preferred_element_type=jnp.float32,
+            )
+            keys = kpos[...]
+            allowed = (keys <= bounds[0, at, :]) & (keys >= bounds[1, at, :])
+            scores = jnp.where(allowed, scores, NEG)
+            peak = jnp.max(scores, axis=-1, keepdims=True)
+            exps = jnp.exp2((scores - peak) * factor)
+            total = jnp.sum(exps, axis=-1, keepdims=True)
+            mixed = jnp.dot(exps.astype(jnp.bfloat16), kv[:, vcol], preferred_element_type=jnp.float32)
+            ocol = pl.ds(pl.multiple_of((first_head + h) * HEAD_SIZE, HEAD_SIZE), HEAD_SIZE)
+            out[at, ocol] = (mixed / total).astype(jnp.bfloat16)
+            return carry
+
+        lax.fori_loop(0, heads * (rows // tile), one, 0)
+
+    x_send(0).wait_recv()
+    y_send(0).start()
+    core_x(0).start()
+    mine = pl.ds(pl.multiple_of(t * rows, rows), rows)
+
+    def block(b, carry):
+        core_send(b).wait_recv()
+
+        def own(i, c):
+            acc[...] += product(b, x_index * 2 + (core + i // 2) % 2, i % 2)
+            return c
+
+        acc[...] = jnp.zeros_like(acc)
+        lax.fori_loop(0, 4, own, 0)
+        core_x(b).wait_recv()
+
+        def crossed(i, c):
+            acc[...] += product(b, (1 - x_index) * 2 + (core + i) % 2, g)
+            return c
+
+        lax.fori_loop(0, 2, crossed, 0)
+
+        @pl.when(b + 1 < blocks)
+        def _():
+            x_send(b + 1).wait_recv()
+            y_send(b + 1).start()
+            core_x(b + 1).start()
+
+        @pl.when(b + AHEAD < blocks)
+        def _():
+            x_send(b + AHEAD).start()
+            core_send(b + AHEAD).start()
+
+        @pl.when(b == kv_blocks)
+        def _():
+            kv_copy(1, t, x_dev).wait_recv()
+            kv_copy(2, t_x, core_dev).start()
+
+        y_send(b).wait_recv()
+        core_y(b).start()
+
+        acc[...] += product(b, t_x, 1 - g)
+        core_y(b).wait_recv()
+        acc[...] += product(b, t_diag, 1 - g)
+
+        @pl.when(b == 0)
+        def _():
+            for head in range(kv_heads):
+                kv[mine, pl.ds(head * HEAD_SIZE, HEAD_SIZE)] = turned(head)
+
+        @pl.when(b == 1)
+        def _():
+            kv[mine, pl.ds(kv_cols, kv_cols)] = acc[...].astype(jnp.bfloat16)
+            kv_copy(1, t, x_dev).start()
+            kv_copy(0, t, core_dev).start()
+
+        @pl.when(b == kv_blocks)
+        def _():
+            kv_copy(0, t, core_dev).wait_recv()
+            kv_copy(2, t_x, core_dev).wait_recv()
+
+        @pl.when(b >= kv_blocks)
+        def _():
+            for head in range(BLOCK // HEAD_SIZE):
+                qrot[:, pl.ds(head * HEAD_SIZE, HEAD_SIZE)] = turned(head)
+            attend(b)
+
+        return carry
+
+    lax.fori_loop(0, blocks, block, 0)
+
+    def drain(b, carry):
+        core_send(b).wait_send()
+        x_send(b).wait_send()
+        y_send(b).wait_send()
+        core_x(b).wait_send()
+        core_y(b).wait_send()
+        return carry
+
+    lax.fori_loop(0, blocks, drain, 0)
+    kv_copy(0, t, core_dev).wait_send()
+    kv_copy(1, t, x_dev).wait_send()
+    kv_copy(2, t_x, core_dev).wait_send()
+
+
+AHEAD = 3
+
+
+def local_fused(tokens, norm_gain, w_query, w_key, value_weight, slab_order, segment_ids):
+    rows, width = tokens.shape
+    slabs = slab_order.shape[0]
+    places = jnp.arange(rows, dtype=jnp.int32)
+    my_position = slab_order[lax.axis_index("ctx")] * rows + places
+    key_positions = (slab_order[:, None] * rows + places[None, :]).reshape(1, slabs * rows)
+    starts = jnp.sum(
+        (segment_ids[None, :] < jnp.arange(1, 4, dtype=jnp.int32)[:, None]).astype(jnp.int32), axis=1
+    )
+    lowest = jnp.max(
+        jnp.where(my_position[:, None] >= starts[None, :], starts[None, :], 0), axis=1
+    )
+    bounds = jnp.stack([my_position, lowest])[:, :, None]
+    half = HEAD_SIZE // 2
+    freqs = jnp.exp(jnp.arange(half, dtype=jnp.float32) * (-2.0 * math.log(500000.0) / HEAD_SIZE))
+    angles = my_position.astype(jnp.float32)[:, None] * freqs[None, :]
+    cosine = jnp.cos(angles)
+    sine = jnp.sin(angles)
+    table = jnp.stack(
+        [jnp.concatenate([cosine, cosine], axis=1), jnp.concatenate([-sine, sine], axis=1)]
+    )
+    shard_rows, query_cols = w_query.shape
+    kv_cols = w_key.shape[1]
+    blocks = (query_cols + 2 * kv_cols) // BLOCK
+    whole = pl.BlockSpec(memory_space=pltpu.VMEM)
+    hbm = pl.BlockSpec(memory_space=pl.ANY)
+    sems = pltpu.SemaphoreType.DMA((blocks,))
+    columns = query_cols + 2 * kv_cols
+    return pl.pallas_call(
+        fused_kernel,
+        out_shape=jax.ShapeDtypeStruct((rows, query_cols), jnp.bfloat16),
+        in_specs=[hbm, whole, hbm, hbm, hbm, whole, whole, whole],
+        out_specs=whole,
+        scratch_shapes=[
+            pltpu.VMEM((blocks, 4, shard_rows, BLOCK), jnp.bfloat16),
+            pltpu.VMEM((rows, width), jnp.bfloat16),
+            pltpu.VMEM((rows, BLOCK), jnp.float32),
+            pltpu.VMEM((rows, BLOCK), jnp.bfloat16),
+            pltpu.VMEM((slabs * rows, 2 * kv_cols), jnp.bfloat16),
+            pltpu.SemaphoreType.DMA((blocks + 1,)),
+            sems, sems, sems, sems, sems, sems, sems, sems, sems, sems,
+            pltpu.SemaphoreType.DMA((3,)),
+            pltpu.SemaphoreType.DMA((3,)),
+        ],
+        compiler_params=pltpu.CompilerParams(
+            collective_id=0, has_side_effects=True, vmem_limit_bytes=58 << 20
+        ),
+        cost_estimate=pl.CostEstimate(
+            flops=2 * rows * width * columns, bytes_accessed=40 << 20, transcendentals=rows * slabs * rows * 8
+        ),
+    )(
+        tokens, norm_gain.reshape(1, width), w_query, w_key, value_weight,
+        table, bounds, key_positions,
+    )
+
+
 def solution(mesh):
+    small = mesh.shape["ctx"] == 4 and mesh.shape["groups"] == 2 and mesh.shape["mp"] == 4
+    local = local_fused if small else local_plain
     return jax.shard_map(
         local,
         mesh=mesh,

time: 257 us -> 123 us (0.48)
  waiting for transfers between devices: 137 us -> 0 us
  Pallas kernels: 0 us -> 112 us
  matrix products: 48.9 us -> 0 us
  blocking collectives: 20.7 us -> 0 us
  other arithmetic: 22.9 us -> 3.52 us
  between operations: 13.3 us -> 0.7 us
  local copies, waits for them, and re-layouts: 13.2 us -> 6.17 us
    all_gather x3 -> x0, waiting for transfers between devices: 135 us -> none  [the longest x1 92.7 us: local(): lax.all_gather(w_query, 'ctx', axis=0, tiled=True)]
    pallas_call x0 -> x1, Pallas kernels: none -> 112 us  [local_fused(): pl.pallas_call(fused_kernel, out_shape=jax.ShapeDtypeStruct((rows, query_...]
    dot_general x9 -> x0, matrix products: 48.9 us -> none  [the longest x3 12.5 us: advance(): jnp.einsum('kgtn,nkd->kgtd', exps.astype(jnp.bfloat16), value_block, pref...]
    all_gather x2 -> x0, blocking collectives: 20.7 us -> none  [the longest x1 11.9 us: local(): key_piece = lax.all_gather(key_rotary, 'ctx', axis=0, tiled=True)]
    reduce_sum x4 -> x1, other arithmetic: 18.4 us -> 0.89 us  [local_fused(): jnp.sum((segment_ids[None, :] < jnp.arange(1, 4, dtype=jnp.int32)[:, None...]
    gather x2 -> x0, local copies, waits for them, and re-layouts: 8.4 us -> none  [local(): segment_all = jnp.take(segment_ids, position_all)]
  transfers between devices with their start and end apart: 3 -> 0, of which waited for: 3 -> 0; matrix products, arithmetic and copies ran while one was open for 11% -> 0% of each run, Pallas kernels for 0% -> 0%
where the time goes in v1:
time: 123 us; the launch traced here: 122 us
  Pallas kernels  112 us (91%)
  local copies, waits for them, and re-layouts  6.17 us (5%)
  other arithmetic  3.52 us (3%)
    pallas_call x1, Pallas kernels, local_fused(): pl.pallas_call(fused_kernel, out_shape=jax.ShapeDtypeStruct((rows, query_...  112 us
    unnamed x2, local copies, waits for them, and re-layouts  2.66 us

profile of v1, /device:TPU:0, one launch (start us, length us, event | category | flops | bytes accessed | tf_op | source)
XLA Modules:
  0.0 122.4 jit_solution(16046544750879141318)
XLA Ops:
  0.0 1.2 %dynamic_slice.3 = s32[1]{0:T(128)} dynamic-slice(s32[4]{0:T(128)} %param.12, s32[]{:T(128)S(6)} %select_n.7), dynamic_slice_sizes={1} | dynamic-slice | bytes 12 | tf_op jit(solution)/shard_map/dynamic_slice | solution.py:350
  1.9 0.7 broadcast_multiply_fusion
  2.6 0.9 convert_reduce_fusion
  3.5 0.1 select_reduce_fusion
  3.6 0.1 add_bitcast_fusion
  3.7 0.6 copy.10
  4.3 1.3 %reshape.55.gain = bf16[1,8192]{1,0:T(2,128)(2,1)} reshape(bf16[8192]{0:T(1024)(128)(2,1)} %param.8) | data formatting | bytes 32768 | tf_op jit(solution)/shard_map/reshape | solution.py:397
  5.6 0.9 copy.9.bounds
  6.5 0.8 multiply_cosine_fusion
  7.3 0.1 maximum_bitcast_fusion
  7.4 0.1 maximum_bitcast_fusion.1
  7.5 0.8 pad_maximum_fusion.table
  8.3 112.0 %shard_map.73 = bf16[384,1024]{1,0:T(8,128)(2,1)} custom-call(bf16[384,8192]{1,0:T(8,128)(2,1)} %tokens.1, bf16[1,8192]{1,0:T(2,128)(2,1)} %reshape.55.gain, bf16[2048,1024]{1,0:T(8,128)(2,1)} %w_query.1, bf16[2048,256]{1,0:T(8,128)(2,1)} %w_key.1, bf16[2048,256]{1,0:T(8,128)(2,1)} %w_value.1, f32[2,384,128]{2,1,0:T(8,128)} %pad_maximum_fusion.table, ...), custom_call_target="tpu_custom_call" | custom-call | flops 9663676416 | bytes 41943040 | tf_op jit(solution)/shard_map/pallas_call | solution.py:374
  120.3 2.1 %copy.12 = bf16[384,1024]{1,0:T(8,128)(2,1)} copy(bf16[384,1024]{1,0:T(8,128)(2,1)} %shard_map.73) | data formatting | bytes 1572864
  (6 shorter events, 0.0 us)
